TPU v7x, 32 devices: a whole 2x2x4 slice. The times are simulated.
32 devices in a mesh: blk: 8 (over y, x, core), col: 4 (over z).
Axes of the slice: x: 2, y: 2, z: 4, core: 2. Of those that a mesh axis runs over, the one named last changes fastest.
Arguments:
- documents: bfloat16 [6144, 768], P('blk'), may hold values from -6 to 6
- landmarks: bfloat16 [4096, 768], P(('blk', 'col')), may hold values from -6 to 6
- eigen_vectors: bfloat16 [4096, 256], P(('blk', 'col')), may hold values from -6 to 6
- land_degree: float32 [4096], P(('blk', 'col')), may hold values from 0.5 to 8
- eigen_values: float32 [256], replicated, may hold values from 0.005 to 0.05
- tile_mask: int32 [48, 32], P('blk'), may hold values from 0 to 1, as said below
- labels: int32 [6144], P(('blk', 'col')), may hold values from 0 to 999
Outputs:
- embedding: float32 [6144, 256], P(('blk', 'col'))
- centroids: float32 [1000, 256], replicated
Inputs may be any that keep to these rules, and one draw needn't show every extreme that they name: `tile_mask`: 1 marks a live tile of 128 documents by 128 landmarks; every document block has at least one live tile.
All inputs are finite; a program needn't handle non-finite values.
Results may differ from a plain program's by a relative error of at most 0.0041.
Values may be sent and summed in bfloat16 or wider, within the bound.
No kernel may reach another device: no remote copies, remote signals or barrier semaphores. Data moves between devices by JAX's collectives and lax.ppermute only.
A program may use at most 64 MiB of HBM per device.

v0:
```python
import jax
import jax.numpy as jnp
from jax import lax
from jax.sharding import PartitionSpec as P

C = 1000
BLOCK = 128


def body(documents, landmarks, eigen_vectors, land_degree, eigen_values, tile_mask, labels):
    inverse_width = 4.0 / documents.shape[1]
    land_rows = landmarks.shape[0]
    col_index = lax.axis_index("col")
    col_count = lax.axis_size("col")
    scaled = (
        eigen_vectors.astype(jnp.float32) * lax.rsqrt(land_degree)[:, None] / eigen_values[None, :]
    ).astype(jnp.bfloat16)
    doc_square = jnp.sum(jnp.square(documents.astype(jnp.float32)), 1)
    land_piece = lax.all_gather(landmarks, "blk", axis=0, tiled=True)
    vector_piece = lax.all_gather(scaled, "blk", axis=0, tiled=True)
    piece_rows = land_piece.shape[0]
    offsets = jnp.arange(piece_rows, dtype=jnp.int32)
    whole_rows = (
        offsets // land_rows * (land_rows * col_count) + col_index * land_rows + offsets % land_rows
    )
    live_cols = jnp.take(tile_mask, whole_rows // BLOCK, axis=1)
    land_square = jnp.sum(jnp.square(land_piece.astype(jnp.float32)), 1)
    products = jnp.einsum("df,lf->dl", documents, land_piece, preferred_element_type=jnp.float32)
    keep = jnp.repeat(live_cols, BLOCK, axis=0).astype(jnp.float32)
    weights = (
        jnp.exp(inverse_width * (2.0 * products - doc_square[:, None] - land_square[None, :]))
        * keep
    )
    total = jnp.dot(weights.astype(jnp.bfloat16), vector_piece, preferred_element_type=jnp.float32)
    projection = total
    degree = jnp.sum(weights, 1)
    projection, degree = (
        lax.psum_scatter(projection, "col", scatter_dimension=0, tiled=True),
        lax.psum_scatter(degree, "col", scatter_dimension=0, tiled=True),
    )
    embedding = projection * lax.rsqrt(degree)[:, None]
    unit_rows = embedding * lax.rsqrt(jnp.sum(jnp.square(embedding), 1, keepdims=True) + 1e-06)
    one_hot = (jnp.arange(C, dtype=jnp.int32)[:, None] == labels[None, :]).astype(jnp.float32)
    partial_sums = jnp.dot(
        one_hot, unit_rows, precision=lax.Precision.HIGHEST, preferred_element_type=jnp.float32
    )
    centroids = lax.psum(partial_sums, ("blk", "col"))
    return (embedding, centroids)


def solution(mesh):
    placed = (
        P("blk", None),
        P(("blk", "col"), None),
        P(("blk", "col"), None),
        P(("blk", "col")),
        P(),
        P("blk", None),
        P(("blk", "col")),
    )
    return jax.shard_map(
        body, mesh=mesh, in_specs=placed, out_specs=(P(("blk", "col"), None), P()), check_vma=False
    )
```

profile of v0, /device:TPU:0, one launch (start us, length us, event | category | flops | bytes accessed | tf_op | source)
XLA Modules:
  0.0 211.5 jit_solution(13693534554832711578)
XLA Ops:
  7.2 0.0 copy-start.6
  7.2 0.0 copy-start.4
  7.2 0.0 copy-start.3
  7.2 0.0 copy-start.1
  7.2 0.0 all-gather.2.cloned.1.call-start
  7.2 0.7 all-gather.2.cloned.1.call-update
  7.9 0.0 reduce-scatter.2.cloned.1.call-start
  8.0 0.8 copy.13
  8.8 2.8 %gather_fusion = s32[1024,6]{1,0:T(8,128)S(1)} fusion(s32[6,32]{0,1:T(8,128)S(1)} %copy.13, s32[1024]{0:T(1024)S(1)} %broadcast_clamp_fusion), kind=kCustom, calls=%fused_computation | custom fusion | bytes 53248 | tf_op jit(solution)/shard_map/jit(_take)/gather | solution.py:26
  11.7 0.2 convert_bitcast_fusion
  11.9 0.2 copy.14
  12.0 0.0 copy-done.6
  12.1 0.0 copy-done.4
  12.1 0.0 copy-done.3
  12.1 0.1 divide_convert_fusion
  12.2 11.3 %all_gather.7 = bf16[1024,256]{1,0:T(8,128)(2,1)S(1)} all-gather(bf16[128,256]{1,0:T(8,128)(2,1)S(1)} %divide_convert_fusion), channel_id=1, replica_groups=mesh['blk'=8,'col'=4] {'blk'}, dimensions={0}, use_global_device_ids=true | all-gather | bytes 589824 | tf_op jit(solution)/shard_map/all_gather | solution.py:20
  23.5 0.0 copy-done.1
  23.5 0.3 multiply_reduce_fusion.1
  23.8 14.6 %all-gather.2.cloned.1.call-done = bf16[1024,768]{1,0:T(8,128)(2,1)} async-done(((bf16[128,768]{1,0:T(8,128)(2,1)}), bf16[1024,768]{1,0:T(8,128)(2,1)}) %all-gather.2.cloned.1.call-update) | async-done | bytes 1572880 | tf_op jit(solution)/shard_map/all_gather | solution.py:19
  38.4 0.0 copy-start
  38.4 1.9 multiply_reduce_fusion
  40.3 0.0 copy-done
  40.3 1.8 fusion
  42.1 0.0 copy-start.7
  42.1 0.0 copy-start.5
  42.1 1.5 fusion.21
  43.6 0.0 reduce-scatter.2.cloned.1.call-update
  43.6 0.0 all-reduce.3.cloned.1.call-start
  43.7 0.0 copy-done.7
  43.7 0.6 dynamic-slice
  44.9 12.0 %all-reduce = f32[768]{0:T(1024)S(1)} all-reduce(f32[768]{0:T(1024)S(1)} %get-tuple-element.4), channel_id=3, replica_groups=mesh['blk'=8,'col'=4] {'col'}, use_global_device_ids=true, to_apply=%region_4.5.clone | all-reduce | flops 768 | bytes 6144
  56.9 0.1 dynamic-slice_rsqrt_fusion
  57.0 10.1 %reduce-scatter.2.cloned.1.call-done = f32[192,256]{1,0:T(8,128)} async-done(((f32[768,256]{1,0:T(8,128)}), f32[192,256]{1,0:T(8,128)}) %reduce-scatter.2.cloned.1.call-update) | async-done | bytes 196624 | tf_op jit(solution)/shard_map/reduce_scatter | solution.py:38
  67.1 1.1 multiply_reduce_fusion.2
  68.2 0.0 copy-start.2
  68.2 0.0 copy-done.5
  68.2 1.6 fusion.2
  69.9 0.0 all-reduce.3.cloned.1.call-update
  69.9 132.8 %all-reduce.3.cloned.1.call-done = f32[1000,256]{1,0:T(8,128)} async-done(((f32[1000,256]{1,0:T(8,128)}), f32[1000,256]{1,0:T(8,128)}) %all-reduce.3.cloned.1.call-update) | async-done | bytes 1024016 | tf_op jit(solution)/shard_map/psum | solution.py:47
  202.7 2.2 %copy.16 = f32[1000,256]{1,0:T(8,128)} copy(f32[1000,256]{1,0:T(8,128)} %all-reduce.3.cloned.1.call-done) | data formatting | bytes 2048000
  205.0 0.0 copy-done.2
  (5 shorter events, 0.1 us)
Async XLA Ops:
  7.2 4.9 %copy-start.6 = (f32[128]{0:T(128)S(1)}, f32[128]{0:T(128)}, u32[]{:S(2)}) copy-start(f32[128]{0:T(128)} %param.10) | copy-start | bytes 1540
  7.2 4.9 %copy-start.4 = (f32[256]{0:T(256)S(1)}, f32[256]{0:T(256)}, u32[]{:S(2)}) copy-start(f32[256]{0:T(256)} %param.11) | copy-start | bytes 3076
  7.2 4.9 %copy-start.3 = (bf16[128,256]{1,0:T(8,128)(2,1)S(1)}, bf16[128,256]{1,0:T(8,128)(2,1)}, u32[]{:S(2)}) copy-start(bf16[128,256]{1,0:T(8,128)(2,1)} %param.9) | copy-start | bytes 196612
  7.2 16.3 %copy-start.1 = (bf16[768,768]{1,0:T(8,128)(2,1)S(1)}, bf16[768,768]{1,0:T(8,128)(2,1)}, u32[]{:S(2)}) copy-start(bf16[768,768]{1,0:T(8,128)(2,1)} %param.7) | copy-start | bytes 3538948
  7.2 31.2 %all-gather.2.cloned.1.call-start = ((), (), s32[]{:S(2)}) async-start(), calls=%async_computation.1 | async-start | bytes 1769472 | tf_op jit(solution)/shard_map/all_gather | solution.py:19
  7.9 59.2 %reduce-scatter.2.cloned.1.call-start = ((), (), s32[]{:S(2)}) async-start(), calls=%async_computation.2 | async-start | bytes 983040 | tf_op jit(solution)/shard_map/reduce_scatter | solution.py:38
  38.4 1.9 copy-start
  42.1 1.6 copy-start.7
  42.1 26.1 %copy-start.5 = (s32[192]{0:T(256)S(1)}, s32[192]{0:T(256)}, u32[]{:S(2)}) copy-start(s32[192]{0:T(256)} %param.13) | copy-start | bytes 2308
  43.6 159.1 %all-reduce.3.cloned.1.call-start = ((), (), s32[]{:S(2)}) async-start(), calls=%async_computation.3 | async-start | bytes 2048000 | tf_op jit(solution)/shard_map/psum | solution.py:47
  68.2 136.8 %copy-start.2 = (f32[192,256]{1,0:T(8,128)}, f32[192,256]{1,0:T(8,128)S(1)}, u32[]{:S(2)}) copy-start(f32[192,256]{1,0:T(8,128)S(1)} %get-tuple-element.6) | copy-start | bytes 589828
Sparse Core Ops, SparseCore 0:
  9.9 28.4 all-gather.1
  43.8 23.2 reduce-scatter.1
  72.8 129.8 all-reduce.2
where the time goes:
time: 212 us
  waiting for transfers between devices  158 us (75%)
  blocking collectives  23.3 us (11%)
  between operations  14.6 us (7%)
  local copies, waits for them, and re-layouts  6.71 us (3%)
  matrix products  4.9 us (2%)
  other arithmetic  3.66 us (2%)
    psum x1, waiting for transfers between devices, body(): centroids = lax.psum(partial_sums, ('blk', 'col'))  133 us
    all_gather x1, waiting for transfers between devices, body(): land_piece = lax.all_gather(landmarks, 'blk', axis=0, tiled=True)  14.6 us
    unnamed x1, blocking collectives  12 us
    all_gather x1, blocking collectives, body(): vector_piece = lax.all_gather(scaled, 'blk', axis=0, tiled=True)  11.3 us
    reduce_scatter x1, waiting for transfers between devices, body(): lax.psum_scatter(projection, 'col', scatter_dimension=0, tiled=True)  10.1 us
  transfers between devices with their start and end apart: 3, of which 3 were waited for; matrix products, arithmetic and copies ran while one was open for 2% of the time, Pallas kernels for 0%

commit v1 on v0

--- a/solution.py
+++ b/solution.py
@@ -16,8 +16,11 @@
         eigen_vectors.astype(jnp.float32) * lax.rsqrt(land_degree)[:, None] / eigen_values[None, :]
     ).astype(jnp.bfloat16)
     doc_square = jnp.sum(jnp.square(documents.astype(jnp.float32)), 1)
-    land_piece = lax.all_gather(landmarks, "blk", axis=0, tiled=True)
-    vector_piece = lax.all_gather(scaled, "blk", axis=0, tiled=True)
+    land_piece, vector_piece = jnp.split(
+        jax.lax.all_gather(jnp.concatenate([landmarks, scaled], axis=1), "blk", axis=0, tiled=True),
+        [landmarks.shape[1]],
+        axis=1,
+    )
     piece_rows = land_piece.shape[0]
     offsets = jnp.arange(piece_rows, dtype=jnp.int32)
     whole_rows = (

time: 212 us -> 218 us (1.028)
  blocking collectives: 23.3 us -> 12 us
  waiting for transfers between devices: 158 us -> 165 us
  other arithmetic: 3.66 us -> 7.41 us
  matrix products: 4.9 us -> 8.3 us
  local copies, waits for them, and re-layouts: 6.71 us -> 10.1 us
    all_gather x1 -> x0, blocking collectives: 11.3 us -> none  [body(): vector_piece = lax.all_gather(scaled, 'blk', axis=0, tiled=True)]
    all_gather x1, waiting for transfers between devices: 14.6 us -> 22.1 us  [body(): jax.lax.all_gather(jnp.concatenate([landmarks, scaled], axis=1), 'blk', a...]
    convert_element_type x1 -> x2, local copies, waits for them, and re-layouts: 0.19 us -> 2.55 us  [body(): keep = jnp.repeat(live_cols, BLOCK, axis=0).astype(jnp.float32)]
    dot_general x1, matrix products: 1.8 us -> 4.12 us  [body(): jnp.einsum('df,lf->dl', documents, land_piece, preferred_element_type=jnp...]
  transfers between devices with their start and end apart: 3 -> 3, of which waited for: 3 -> 3; matrix products, arithmetic and copies ran while one was open for 2% -> 4% of each run, Pallas kernels for 0% -> 0%
where the time goes in v1:
time: 218 us
  waiting for transfers between devices  165 us (76%)
  between operations  14.5 us (7%)
  blocking collectives  12 us (6%)
  local copies, waits for them, and re-layouts  10.1 us (5%)
  matrix products  8.3 us (4%)
  other arithmetic  7.41 us (3%)
    psum x1, waiting for transfers between devices, body(): centroids = lax.psum(partial_sums, ('blk', 'col'))  133 us
    all_gather x1, waiting for transfers between devices, body(): jax.lax.all_gather(jnp.concatenate([landmarks, scaled], axis=1), 'blk', a...  22.1 us
    unnamed x1, blocking collectives  12 us
    reduce_scatter x1, waiting for transfers between devices, body(): lax.psum_scatter(projection, 'col', scatter_dimension=0, tiled=True)  10 us
  transfers between devices with their start and end apart: 3, of which 3 were waited for; matrix products, arithmetic and copies ran while one was open for 4% of the time, Pallas kernels for 0%

profile of v1, /device:TPU:0, one launch (start us, length us, event | category | flops | bytes accessed | tf_op | source)
XLA Modules:
  0.0 217.5 jit_solution(15986826658632600904)
XLA Ops:
  7.2 0.0 all-gather.2.cloned.1.call-start
  7.2 0.7 rsqrt.14
  7.9 0.9 divide_convert_fusion
  8.8 1.7 pad_maximum_fusion
  10.5 0.0 all-gather.2.cloned.1.call-update
  10.5 0.0 reduce-scatter.2.cloned.1.call-start
  10.5 0.8 copy.13
  11.4 2.8 %gather_fusion = s32[1024,6]{1,0:T(8,128)S(1)} fusion(s32[6,32]{0,1:T(8,128)S(1)} %copy.13, s32[1024]{0:T(1024)S(1)} %broadcast_clamp_fusion), kind=kCustom, calls=%fused_computation | custom fusion | bytes 53248 | tf_op jit(solution)/shard_map/jit(_take)/gather | solution.py:29
  14.2 0.2 convert_bitcast_fusion
  14.4 0.2 copy.14
  14.6 0.4 broadcast_in_dim.14
  15.0 2.4 %copy.15 = f32[768,1024]{0,1:T(8,128)} copy(f32[768,1024]{1,0:T(8,128)S(1)} %bitcast.9) | data formatting | bytes 6291456 | tf_op jit(solution)/shard_map/convert_element_type | solution.py:32
  17.4 0.0 copy-start
  17.4 1.7 multiply_reduce_fusion.1
  19.0 22.1 %all-gather.2.cloned.1.call-done = bf16[1024,1024]{1,0:T(8,128)(2,1)} async-done(((bf16[128,1024]{1,0:T(8,128)(2,1)}), bf16[1024,1024]{1,0:T(8,128)(2,1)}) %all-gather.2.cloned.1.call-update) | async-done | bytes 2097168 | tf_op jit(solution)/shard_map/all_gather | solution.py:20
  41.1 1.8 multiply_reduce_fusion
  42.9 0.0 copy-done
  42.9 4.1 %fusion.23 = (f32[768]{0:T(1024)S(1)}, bf16[768,1024]{0,1:T(8,128)(2,1)S(1)}) fusion(f32[768,1024]{0,1:T(8,128)} %copy.15, f32[1024]{0:T(1024)S(1)} %multiply_reduce_fusion, f32[768]{0:T(1024)S(1)} %multiply_reduce_fusion.1, bf16[768,768]{1,0:T(8,128)(2,1)S(1)} %copy-done, bf16[1024,1024]{1,0:T(8,128)(2,1)} %all-gather.2.cloned.1.call-done), kind=kOutput, calls=%fused_computation.57 | convolution fusion | flops 1213463808 | bytes 7481344 | tf_op jit(solution)/shard_map/df,lf->dl/dot_general | solution.py:31
  47.1 0.0 copy-start.3
  47.1 0.0 copy-start.2
  47.1 2.5 %fusion = f32[768,256]{1,0:T(8,128)} fusion(bf16[768,1024]{0,1:T(8,128)(2,1)S(1)} %get-tuple-element.5, bf16[1024,1024]{1,0:T(8,128)(2,1)} %all-gather.2.cloned.1.call-done), kind=kOutput, calls=%fused_computation.4 | convolution fusion | flops 402653184 | bytes 2883584 | tf_op jit(solution)/shard_map/dot_general | solution.py:37
  49.6 0.0 reduce-scatter.2.cloned.1.call-update
  49.7 0.0 all-reduce.3.cloned.1.call-start
  49.7 0.0 copy-done.3
  49.7 0.6 dynamic-slice
  51.0 12.0 %all-reduce = f32[768]{0:T(1024)S(1)} all-reduce(f32[768]{0:T(1024)S(1)} %get-tuple-element.4), channel_id=3, replica_groups=mesh['blk'=8,'col'=4] {'col'}, use_global_device_ids=true, to_apply=%region_4.5.clone | all-reduce | flops 768 | bytes 6144
  63.0 0.1 dynamic-slice_rsqrt_fusion
  63.1 10.0 %reduce-scatter.2.cloned.1.call-done = f32[192,256]{1,0:T(8,128)} async-done(((f32[768,256]{1,0:T(8,128)}), f32[192,256]{1,0:T(8,128)}) %reduce-scatter.2.cloned.1.call-update) | async-done | bytes 196624 | tf_op jit(solution)/shard_map/reduce_scatter | solution.py:41
  73.1 1.1 multiply_reduce_fusion.2
  74.2 0.0 copy-start.1
  74.2 0.0 copy-done.2
  74.2 1.6 fusion.3
  75.9 0.0 all-reduce.3.cloned.1.call-update
  75.9 132.8 %all-reduce.3.cloned.1.call-done = f32[1000,256]{1,0:T(8,128)} async-done(((f32[1000,256]{1,0:T(8,128)}), f32[1000,256]{1,0:T(8,128)}) %all-reduce.3.cloned.1.call-update) | async-done | bytes 1024016 | tf_op jit(solution)/shard_map/psum | solution.py:50
  208.7 2.2 %copy.17 = f32[1000,256]{1,0:T(8,128)} copy(f32[1000,256]{1,0:T(8,128)} %all-reduce.3.cloned.1.call-done) | data formatting | bytes 2048000
  211.0 0.0 copy-done.1
  (4 shorter events, 0.1 us)
Async XLA Ops:
  7.2 34.0 %all-gather.2.cloned.1.call-start = ((), (), s32[]{:S(2)}) async-start(), calls=%async_computation.1 | async-start | bytes 2359296 | tf_op jit(solution)/shard_map/all_gather | solution.py:20
  10.5 62.6 %reduce-scatter.2.cloned.1.call-start = ((), (), s32[]{:S(2)}) async-start(), calls=%async_computation.2 | async-start | bytes 983040 | tf_op jit(solution)/shard_map/reduce_scatter | solution.py:41
  17.4 25.6 %copy-start = (bf16[768,768]{1,0:T(8,128)(2,1)S(1)}, bf16[768,768]{1,0:T(8,128)(2,1)}, u32[]{:S(2)}) copy-start(bf16[768,768]{1,0:T(8,128)(2,1)} %param.7) | copy-start | bytes 3538948
  47.1 2.6 %copy-start.3 = (u32[32]{0:T(128)S(1)}, u32[32]{0:T(128)}, u32[]{:S(2)}) copy-start(u32[32]{0:T(128)} %constant.75) | copy-start | bytes 388
  47.1 27.1 %copy-start.2 = (s32[192]{0:T(256)S(1)}, s32[192]{0:T(256)}, u32[]{:S(2)}) copy-start(s32[192]{0:T(256)} %param.13) | copy-start | bytes 2308
  49.7 159.1 %all-reduce.3.cloned.1.call-start = ((), (), s32[]{:S(2)}) async-start(), calls=%async_computation.3 | async-start | bytes 2048000 | tf_op jit(solution)/shard_map/psum | solution.py:50
  74.2 136.8 %copy-start.1 = (f32[192,256]{1,0:T(8,128)}, f32[192,256]{1,0:T(8,128)S(1)}, u32[]{:S(2)}) copy-start(f32[192,256]{1,0:T(8,128)S(1)} %get-tuple-element.8) | copy-start | bytes 589828
Sparse Core Ops, SparseCore 0:
  10.6 30.4 all-gather.1
  49.8 23.2 reduce-scatter.1
  78.8 129.8 all-reduce.2
